TPU v7x, 128 devices: a whole 4x4x4 slice. The times are simulated.
128 devices in a mesh: chan: 8 (over x, core), row: 16 (over y, z).
Axes of the slice: x: 4, y: 4, z: 4, core: 2. Of those that a mesh axis runs over, the one named last changes fastest.
Arguments:
- generator: bfloat16 [8, 2560, 2560], P('chan', 'row'), may hold values from -0.06 to 0.06, as said below
- hamiltonian: bfloat16 [8, 2560, 2560], P('chan', 'row'), may hold values from -6 to 6, as said below
- live_states: int32 [8], P('chan'), may hold values from 1 to 2560, 11520 in all
- pp_occupation: int32 [8, 2560], P('chan'), may hold values from -1 to 1
- ph_occupation: int32 [8, 2560], P('chan'), may hold values from -1 to 1
- ph_order: int32 [8, 2560], P('chan'), may hold values from 0 to 2559, as said below
- recoupling: float32 [8, 2], replicated, may hold values from 0.4 to 1
Outputs:
- transformed: float32 [8, 2560, 2560], P('chan', 'row')
Inputs may be any that keep to these rules, and one draw needn't show every extreme that they name: Each generator[c] is antisymmetric. Each hamiltonian[c] is symmetric. Each ph_order[c] is a permutation of 0 to 2559, and entry r * 160 + q * 16 + s, for 0 <= q < 10, lies in [s * 160, (s + 1) * 160).
All inputs are finite; a program needn't handle non-finite values. No bound on the sum of `live_states` on one device may be relied on, other than what follows from the above.
Results may differ from a plain program's by a relative error of at most 0.005.
Values may be sent and summed in bfloat16 or wider, within the bound.
No kernel may reach another device: no remote copies, remote signals or barrier semaphores. Data moves between devices by JAX's collectives and lax.ppermute only.
A program may use at most 128 MiB of HBM per device.

v0:
```python
import jax
import jax.numpy as jnp
from jax import lax
from jax.sharding import Mesh, PartitionSpec as P

TERMS = 3


def swapped(value):
    return lax.ppermute(value, "hi", [(0, 1), (1, 0)])


def on_device(
    generator, hamiltonian, live_states, pp_occupation, ph_occupation, ph_order, recoupling
):
    row_count = generator.shape[1]
    state_count = generator.shape[2]
    half = row_count // 2
    shard_count = lax.axis_size("row")
    hi = lax.axis_index("hi")
    lo = lax.axis_index("lo")
    my_shard = lax.axis_index("row")
    first = hi == 0
    r0 = recoupling[lo]
    r1 = recoupling[lo + lax.axis_size("lo")]
    positions = jnp.arange(state_count, dtype=jnp.int32)
    live_count = live_states[0]
    column_alive = positions < live_count
    row_alive = my_shard * row_count + jnp.arange(row_count, dtype=jnp.int32) < live_count
    block_alive = row_alive[:, None] & column_alive[None, :]
    own_share = jnp.where(block_alive, generator[0], jnp.zeros_like(generator[0]))
    far_share = swapped(own_share)
    full_own = lax.all_gather(own_share, "row", axis=0, tiled=True)
    full_far = lax.all_gather(far_share, "row", axis=0, tiled=True)
    pp = jnp.where(column_alive, pp_occupation[0], 0)
    ph = jnp.zeros((state_count,), jnp.int32).at[ph_order[0]].set(ph_occupation[0])
    ph = jnp.where(column_alive, ph, 0)
    mine = jnp.stack([pp, ph]).astype(jnp.float32)
    other = swapped(mine)
    d0, n0 = jnp.where(first, mine, other)
    d1, n1 = jnp.where(first, other, mine)
    a0 = d0 + r0[0] ** 3 * n0 + r1[1] ** 3 * n1
    a1 = d1 + r1[0] ** 3 * n1 + r0[1] ** 3 * n0
    p = r0[0] ** 2 * r0[1] * n0 + r1[1] ** 2 * r1[0] * n1
    q = r1[0] ** 2 * r1[1] * n1 + r0[1] ** 2 * r0[0] * n0
    zero_set = jnp.stack([a0, p, p, q])
    one_set = jnp.stack([p, q, q, a1])
    own_set = jnp.where(first, zero_set, one_set)
    far_set = jnp.where(first, one_set, zero_set)
    own_ham = jnp.where(block_alive, hamiltonian[0], jnp.zeros_like(hamiltonian[0]))
    keep = lax.dynamic_slice_in_dim(own_ham, hi * half, half, 0)
    gone = lax.dynamic_slice_in_dim(own_ham, (1 - hi) * half, half, 0)
    came = swapped(gone)
    current = jnp.concatenate([jnp.where(first, keep, came), jnp.where(first, came, keep)])
    running = jnp.zeros(current.shape, jnp.float32)

    def mix(x, s):
        x0, x1 = (x[:half], x[half:])
        top = x0 * s[0] + x1 * s[1]
        low = x0 * s[2] + x1 * s[3]
        return jnp.concatenate([top, low]).astype(jnp.bfloat16)

    for term_index in range(1, TERMS + 1):
        wide = current.astype(jnp.float32)
        combined = jnp.dot(
            mix(wide, own_set), full_own, preferred_element_type=jnp.float32
        ) + jnp.dot(mix(wide, far_set), full_far, preferred_element_type=jnp.float32)
        combined = combined.astype(jnp.bfloat16)
        if term_index < TERMS:
            sent = combined.T
            got = lax.all_to_all(sent, ("row", "hi"), split_axis=0, concat_axis=0, tiled=True)
            got = got.reshape(2 * shard_count, half, 2, half)
            flipped = jnp.transpose(got, (2, 1, 0, 3)).reshape(row_count, state_count)
            increment = -(combined.astype(jnp.float32) + flipped.astype(jnp.float32)) / term_index
            running = running + increment
            current = increment.astype(jnp.bfloat16)
    running = running - combined.astype(jnp.float32) / TERMS
    leaving = lax.dynamic_slice_in_dim(running, (1 - hi) * half, half, 0).astype(jnp.bfloat16)
    staying = lax.dynamic_slice_in_dim(running, hi * half, half, 0)
    landed = swapped(leaving).astype(jnp.float32)
    blocks = combined.reshape(2, half, shard_count, row_count)
    blocks = jnp.transpose(blocks, (0, 2, 3, 1)).reshape(2 * state_count, half)
    got = lax.all_to_all(blocks, ("hi", "row"), split_axis=0, concat_axis=0, tiled=True)
    got = got.reshape(2, shard_count, row_count, half)
    flipped = jnp.transpose(got, (2, 1, 0, 3)).reshape(row_count, state_count)
    rows = jnp.concatenate([jnp.where(first, staying, landed), jnp.where(first, landed, staying)])
    return (own_ham.astype(jnp.float32) + rows - flipped.astype(jnp.float32) / TERMS)[None]


def solution(mesh):
    chans, rows = mesh.devices.shape
    pairs = Mesh(mesh.devices.reshape(2, chans // 2, rows), ("hi", "lo", "row"))
    chan = ("hi", "lo")
    placed = (
        P(chan, "row", None),
        P(chan, "row", None),
        P(chan),
        P(chan, None),
        P(chan, None),
        P(chan, None),
        P(),
    )
    return jax.shard_map(
        on_device, mesh=pairs, in_specs=placed, out_specs=P(chan, "row", None), check_vma=False
    )
```

profile of v0, /device:TPU:0, one launch (start us, length us, event | category | flops | bytes accessed | tf_op | source)
XLA Modules:
  0.0 352.6 jit_solution(11028163509748805113)
XLA Ops:
  7.2 2.8 and_select_fusion.1
  10.1 3.2 collective-permute-start.2
  13.3 18.5 %collective-permute-done.2 = bf16[160,2560]{1,0:T(8,128)(2,1)S(1)} collective-permute-done((bf16[160,2560]{1,0:T(8,128)(2,1)}, bf16[160,2560]{1,0:T(8,128)(2,1)S(1)}, u32[]{:S(2)}, u32[]{:S(2)}) %collective-permute-start.2) | collective-permute-done | bytes 819232 | tf_op jit(solution)/shard_map/ppermute | solution.py:10
  32.7 9.9 %scatter_custom_fusion = s32[2560]{0:T(1024)S(1)} fusion(s32[2560]{0:T(1024)S(1)} %fusion.31, s32[2560]{0:T(1024)S(1)} %reduce.1, s32[]{:T(128)} %constant.13.clone.1), kind=kCustom, calls=%fused_computation.88 | custom fusion | bytes 10244 | tf_op jit(solution)/shard_map/scatter | solution.py:36
  42.8 3.3 collective-permute-start.1
  58.6 46.6 %all-gather.3.cloned.1.call-done = bf16[2560,2560]{1,0:T(8,128)(2,1)} async-done(((bf16[160,2560]{1,0:T(8,128)(2,1)}), bf16[2560,2560]{1,0:T(8,128)(2,1)}) %all-gather.3.cloned.1.call-update) | async-done | bytes 13107216 | tf_op jit(solution)/shard_map/all_gather | solution.py:33
  105.2 8.2 %fusion.10 = f32[160,2560]{1,0:T(8,128)} fusion(bf16[2560,2560]{1,0:T(8,128)(2,1)} %all-gather.3.cloned.1.call-done, bf16[80,2560]{1,0:T(8,128)(2,1)S(1)} %get-tuple-element.26, bf16[80,2560]{1,0:T(8,128)(2,1)S(1)} %get-tuple-element.25), kind=kOutput, calls=%fused_computation.26 | convolution fusion | flops 2098790400 | bytes 15564800 | tf_op jit(solution)/shard_map/dot_general | solution.py:65
  113.4 86.2 %all-gather.5.cloned.1.call-done = bf16[2560,2560]{1,0:T(8,128)(2,1)} async-done(((bf16[160,2560]{1,0:T(8,128)(2,1)}), bf16[2560,2560]{1,0:T(8,128)(2,1)}) %all-gather.5.cloned.1.call-update) | async-done | bytes 13107216 | tf_op jit(solution)/shard_map/all_gather | solution.py:34
  199.6 7.5 %fusion = bf16[160,2560]{1,0:T(8,128)(2,1)S(1)} fusion(f32[160,2560]{1,0:T(8,128)} %fusion.10, bf16[2560,2560]{1,0:T(8,128)(2,1)} %all-gather.5.cloned.1.call-done, bf16[80,2560]{1,0:T(8,128)(2,1)S(1)} %get-tuple-element.24, bf16[80,2560]{1,0:T(8,128)(2,1)S(1)} %get-tuple-element.23), kind=kOutput, calls=%fused_computation.4 | convolution fusion | flops 2099609600 | bytes 16384000 | tf_op jit(solution)/shard_map/dot_general | solution.py:67
  207.1 1.6 all_to_all.18
  209.3 29.8 %all_to_all.27 = bf16[32,80,160]{1,2,0:T(8,128)(2,1)S(1)} all-to-all(bf16[32,80,160]{1,2,0:T(8,128)(2,1)S(1)} %copy.14), channel_id=1, replica_groups=mesh['hi'=2,'lo'=4,'row'=16] {'row','hi'}, dimensions={0} | all-to-all | bytes 1638400 | tf_op jit(solution)/shard_map/all_to_all | solution.py:71
  239.1 2.7 copy.15
  241.7 2.9 reshape.143
  245.3 7.3 %fusion.17 = f32[160,2560]{1,0:T(8,128)S(1)} fusion(bf16[2560,2560]{1,0:T(8,128)(2,1)} %all-gather.3.cloned.1.call-done, bf16[80,2560]{1,0:T(8,128)(2,1)S(1)} %get-tuple-element.22, bf16[80,2560]{1,0:T(8,128)(2,1)S(1)} %get-tuple-element.21), kind=kOutput, calls=%fused_computation.33 | convolution fusion | flops 2098790400 | bytes 15564800 | tf_op jit(solution)/shard_map/dot_general | solution.py:65
  253.2 2.3 fusion.1
  255.5 2.4 all_to_all.20
  258.0 1.8 copy.16
  259.8 24.2 %all_to_all.28 = bf16[32,80,160]{1,2,0:T(8,128)(2,1)S(1)} all-to-all(bf16[32,80,160]{1,2,0:T(8,128)(2,1)S(1)} %copy.16), channel_id=1, replica_groups=mesh['hi'=2,'lo'=4,'row'=16] {'row','hi'}, dimensions={0} | all-to-all | bytes 1638400 | tf_op jit(solution)/shard_map/all_to_all | solution.py:71
  284.0 1.8 convert_bitcast_fusion
  285.8 4.3 %copy.17 = f32[2,80,32,80]{3,2,1,0:T(8,128)} copy(f32[2,80,32,80]{1,3,0,2:T(8,128)} %convert_bitcast_fusion) | data formatting | bytes 3276800 | tf_op jit(solution)/shard_map/convert_element_type | solution.py:74
  290.1 2.9 reshape.144
  293.1 1.5 fusion.6
  295.0 7.2 %fusion.24 = f32[160,2560]{1,0:T(8,128)S(1)} fusion(bf16[2560,2560]{1,0:T(8,128)(2,1)} %all-gather.3.cloned.1.call-done, bf16[80,2560]{1,0:T(8,128)(2,1)S(1)} %get-tuple-element.18, bf16[80,2560]{1,0:T(8,128)(2,1)S(1)} %get-tuple-element.17), kind=kOutput, calls=%fused_computation.40 | convolution fusion | flops 2098790400 | bytes 15564800 | tf_op jit(solution)/shard_map/dot_general | solution.py:65
  302.4 3.5 multiply_subtract_fusion
  307.0 2.6 reshape.142
  309.6 2.3 copy.18
  311.9 6.0 %all-to-all-start.2 = ((bf16[32,160,80]{2,1,0:T(8,128)(2,1)}), bf16[32,160,80]{2,1,0:T(8,128)(2,1)S(1)}, u32[]{:S(2)}, u32[]{:S(2)}) async-start(bf16[32,160,80]{2,1,0:T(8,128)(2,1)} %bitcast.17), calls=%async_computation.2 | async-start | bytes 2621440 | tf_op jit(solution)/shard_map/all_to_all | solution.py:83
  317.9 2.4 fusion.7
  320.3 14.9 %all-to-all-done.2 = bf16[32,160,80]{2,1,0:T(8,128)(2,1)S(1)} async-done(((bf16[32,160,80]{2,1,0:T(8,128)(2,1)}), bf16[32,160,80]{2,1,0:T(8,128)(2,1)S(1)}, u32[]{:S(2)}, u32[]{:S(2)}) %all-to-all-start.2) | async-done | bytes 819232 | tf_op jit(solution)/shard_map/all_to_all | solution.py:83
  335.5 2.0 copy.19
  337.6 4.7 %div.26 = f32[1,160,2560]{2,1,0:T(8,128)} reshape(f32[160,16,2,80]{3,2,1,0:T(2,128)S(1)} %copy.19) | data formatting | bytes 3276800 | tf_op jit(solution)/shard_map/div | solution.py:87
  342.3 3.5 fusion.3
  (76 shorter events, 7.3 us)
Async XLA Ops:
  6.5 98.7 %all-gather.3.cloned.1.call-start = ((), (), s32[]{:S(2)}) async-start(), calls=%async_computation.3 | async-start | bytes 13926400 | tf_op jit(solution)/shard_map/all_gather | solution.py:33
  10.0 22.7 %copy-start.8 = (s32[1,2560]{1,0:T(1,128)S(1)}, s32[1,2560]{1,0:T(1,128)}, u32[]{:S(2)}) copy-start(s32[1,2560]{1,0:T(1,128)} %param.11) | copy-start | bytes 30724
  10.0 22.7 %copy-start.9 = (s32[1,2560]{1,0:T(1,128)S(1)}, s32[1,2560]{1,0:T(1,128)}, u32[]{:S(2)}) copy-start(s32[1,2560]{1,0:T(1,128)} %param.12) | copy-start | bytes 30724
  10.0 32.7 %copy-start.10 = (s32[1,2560]{1,0:T(1,128)S(1)}, s32[1,2560]{1,0:T(1,128)}, u32[]{:S(2)}) copy-start(s32[1,2560]{1,0:T(1,128)} %param.10) | copy-start | bytes 30724
  10.0 36.5 %copy-start.11 = (f32[8,2]{0,1:T(2,128)S(1)}, f32[8,2]{0,1:T(2,128)}, u32[]{:S(2)}) copy-start(f32[8,2]{0,1:T(2,128)} %param.13) | copy-start | bytes 196
  10.0 189.6 %all-gather.5.cloned.1.call-start = ((), (), s32[]{:S(2)}) async-start(), calls=%async_computation.4 | async-start | bytes 13926400 | tf_op jit(solution)/shard_map/all_gather | solution.py:34
  10.1 21.7 %collective-permute-start.2 = (bf16[160,2560]{1,0:T(8,128)(2,1)}, bf16[160,2560]{1,0:T(8,128)(2,1)S(1)}, u32[]{:S(2)}, u32[]{:S(2)}) collective-permute-start(bf16[160,2560]{1,0:T(8,128)(2,1)} %get-tuple-element.38), channel_id=1, source_target_pairs={{0,64},{64,0},{1,65},{65,1},{2,66},{66,2},{3,67},{67,3},{4,68},{68... | collective-permute-start | bytes 2457608 | tf_op jit(solution)/shard_map/ppermute | solution.py:10
  31.7 0.9 copy-start.7
  42.8 14.3 %collective-permute-start.1 = (f32[2,2560]{1,0:T(2,128)S(1)}, f32[2,2560]{1,0:T(2,128)S(1)}, u32[]{:S(2)}, u32[]{:S(2)}) collective-permute-start(f32[2,2560]{1,0:T(2,128)S(1)} %add_convert_fusion.12), channel_id=1, source_target_pairs={{0,64},{64,0},{1,65},{65,1},{2,66},{66,2},{3,67},{67,3},{4,68},{68... | collective-permute-start | bytes 61448 | tf_op jit(solution)/shard_map/ppermute | solution.py:10
  46.1 11.8 %collective-permute-start = (bf16[80,2560]{1,0:T(8,128)(2,1)S(1)}, bf16[80,2560]{1,0:T(8,128)(2,1)S(1)}, u32[]{:S(2)}, u32[]{:S(2)}) collective-permute-start(bf16[80,2560]{1,0:T(8,128)(2,1)S(1)} %constant_dynamic-slice_fusion.2), channel_id=1, source_target_pairs={{0,64},{64,0},{1,65},{65,1},{2,66},{66,2},{3,67},{67,3},{4,68},{68... | collective-permute-start | bytes 1228808 | tf_op jit(solution)/shard_map/ppermute | solution.py:10
  207.1 37.5 %copy-start = (bf16[160,2560]{1,0:T(8,128)(2,1)}, bf16[160,2560]{1,0:T(8,128)(2,1)S(1)}, u32[]{:S(2)}) copy-start(bf16[160,2560]{1,0:T(8,128)(2,1)S(1)} %fusion) | copy-start | bytes 2457604
  244.7 8.0 %slice-start = ((s8[13107200]{0:T(1024)(128)(4,1)}), s8[4194304]{0:T(1024)(128)(4,1)S(1)}, s32[]{:S(2)}) async-start(s8[13107200]{0:T(1024)(128)(4,1)} %bitcast.49), calls=%async_computation.5 | async-start | bytes 8388608
  244.9 7.8 %slice-start.1 = ((s8[13107200]{0:T(1024)(128)(4,1)}), s8[4194304]{0:T(1024)(128)(4,1)S(1)}, s32[]{:S(2)}) async-start(s8[13107200]{0:T(1024)(128)(4,1)} %bitcast.49), calls=%async_computation.6 | async-start | bytes 8388608
  245.3 7.9 %slice-start.2 = ((s8[13107200]{0:T(1024)(128)(4,1)}), s8[4194304]{0:T(1024)(128)(4,1)S(1)}, s32[]{:S(2)}) async-start(s8[13107200]{0:T(1024)(128)(4,1)} %bitcast.49), calls=%async_computation.7 | async-start | bytes 8388608
  245.3 7.9 %slice-start.3 = ((s8[13107200]{0:T(1024)(128)(4,1)}), s8[524288]{0:T(1024)(128)(4,1)S(1)}, s32[]{:S(2)}) async-start(s8[13107200]{0:T(1024)(128)(4,1)} %bitcast.49), calls=%async_computation.8 | async-start | bytes 1048576
  255.5 4.3 %copy-start.2 = (bf16[160,2560]{1,0:T(8,128)(2,1)}, bf16[160,2560]{1,0:T(8,128)(2,1)S(1)}, u32[]{:S(2)}) copy-start(bf16[160,2560]{1,0:T(8,128)(2,1)S(1)} %fusion.1) | copy-start | bytes 2457604
  293.0 9.2 %slice-start.4 = ((s8[13107200]{0:T(1024)(128)(4,1)}), s8[4194304]{0:T(1024)(128)(4,1)S(1)}, s32[]{:S(2)}) async-start(s8[13107200]{0:T(1024)(128)(4,1)} %bitcast.51), calls=%async_computation.9 | async-start | bytes 8388608
  294.6 7.7 %slice-start.5 = ((s8[13107200]{0:T(1024)(128)(4,1)}), s8[4194304]{0:T(1024)(128)(4,1)S(1)}, s32[]{:S(2)}) async-start(s8[13107200]{0:T(1024)(128)(4,1)} %bitcast.51), calls=%async_computation.10 | async-start | bytes 8388608
  295.0 7.3 %slice-start.6 = ((s8[13107200]{0:T(1024)(128)(4,1)}), s8[4194304]{0:T(1024)(128)(4,1)S(1)}, s32[]{:S(2)}) async-start(s8[13107200]{0:T(1024)(128)(4,1)} %bitcast.51), calls=%async_computation.11 | async-start | bytes 8388608
  295.0 7.3 %slice-start.7 = ((s8[13107200]{0:T(1024)(128)(4,1)}), s8[524288]{0:T(1024)(128)(4,1)S(1)}, s32[]{:S(2)}) async-start(s8[13107200]{0:T(1024)(128)(4,1)} %bitcast.51), calls=%async_computation.12 | async-start | bytes 1048576
  295.0 7.3 %copy-start.1 = (bf16[160,2560]{1,0:T(8,128)(2,1)S(1)}, bf16[160,2560]{1,0:T(8,128)(2,1)}, u32[]{:S(2)}) copy-start(bf16[160,2560]{1,0:T(8,128)(2,1)} %copy-done) | copy-start | bytes 2457604
  295.0 7.4 %copy-start.3 = (bf16[160,2560]{1,0:T(8,128)(2,1)S(1)}, bf16[160,2560]{1,0:T(8,128)(2,1)}, u32[]{:S(2)}) copy-start(bf16[160,2560]{1,0:T(8,128)(2,1)} %copy-done.2) | copy-start | bytes 2457604
  305.9 1.2 copy-start.4
  305.9 12.0 %collective-permute-start.3 = (bf16[80,2560]{1,0:T(8,128)(2,1)S(1)}, bf16[80,2560]{1,0:T(8,128)(2,1)}, u32[]{:S(2)}, u32[]{:S(2)}) collective-permute-start(bf16[80,2560]{1,0:T(8,128)(2,1)S(1)} %dynamic-slice_convert_fusion), channel_id=1, source_target_pairs={{0,64},{64,0},{1,65},{65,1},{2,66},{66,2},{3,67},{67,3},{4,68},{68... | collective-permute-start | bytes 1228808 | tf_op jit(solution)/shard_map/ppermute | solution.py:10
  311.9 6.0 %copy-start.5 = (f32[160,2560]{1,0:T(8,128)S(1)}, f32[160,2560]{1,0:T(8,128)}, u32[]{:S(2)}) copy-start(f32[160,2560]{1,0:T(8,128)} %copy-done.4) | copy-start | bytes 4915204
  311.9 23.3 %all-to-all-start.2 = ((bf16[32,160,80]{2,1,0:T(8,128)(2,1)}), bf16[32,160,80]{2,1,0:T(8,128)(2,1)S(1)}, u32[]{:S(2)}, u32[]{:S(2)}) async-start(bf16[32,160,80]{2,1,0:T(8,128)(2,1)} %bitcast.17), calls=%async_computation.2 | async-start | bytes 2621440 | tf_op jit(solution)/shard_map/all_to_all | solution.py:83
  337.6 4.7 %copy-start.6 = (bf16[1,160,2560]{2,1,0:T(8,128)(2,1)S(1)}, bf16[1,160,2560]{2,1,0:T(8,128)(2,1)}, u32[]{:S(2)}) copy-start(bf16[1,160,2560]{2,1,0:T(8,128)(2,1)} %param.8) | copy-start | bytes 2457604
Sparse Core Ops, SparseCore 0:
  10.1 95.0 all-gather.2
  107.4 92.1 all-gather.4
where the time goes:
time: 353 us
  waiting for transfers between devices  167 us (47%)
  blocking collectives  54 us (15%)
  local copies, waits for them, and re-layouts  43.7 us (12%)
  matrix products  36 us (10%)
  between operations  24.5 us (7%)
  other arithmetic  14.2 us (4%)
  starting transfers between devices  13.6 us (4%)
    all_gather x1, waiting for transfers between devices, on_device(): full_far = lax.all_gather(far_share, 'row', axis=0, tiled=True)  86.2 us
    all_to_all x2, blocking collectives, on_device(): lax.all_to_all(sent, ('row', 'hi'), split_axis=0, concat_axis=0, tiled=True)  54 us
    all_gather x1, waiting for transfers between devices, on_device(): full_own = lax.all_gather(own_share, 'row', axis=0, tiled=True)  46.6 us
    dot_general x3, matrix products, on_device(): jnp.dot(mix(wide, own_set), full_own, preferred_element_type=jnp.float32)  22.7 us
    ppermute x4, waiting for transfers between devices, swapped(): return lax.ppermute(value, 'hi', [(0, 1), (1, 0)])  18.8 us
    all_to_all x1, waiting for transfers between devices, on_device(): lax.all_to_all(blocks, ('hi', 'row'), split_axis=0, concat_axis=0, tiled=...  14.9 us
    dot_general x3, matrix products, on_device(): jnp.dot(mix(wide, far_set), full_far, preferred_element_type=jnp.float32)  13.3 us
    convert_element_type x4, local copies, waits for them, and re-layouts, on_device(): flipped.astype(jnp.float32)  12.8 us
  transfers between devices with their start and end apart: 7, of which 5 were waited for; matrix products, arithmetic and copies ran while one was open for 8% of the time, Pallas kernels for 0%

commit v1 on v0

--- a/solution.py
+++ b/solution.py
@@ -31,7 +31,9 @@
     own_share = jnp.where(block_alive, generator[0], jnp.zeros_like(generator[0]))
     far_share = swapped(own_share)
     full_own = lax.all_gather(own_share, "row", axis=0, tiled=True)
-    full_far = lax.all_gather(far_share, "row", axis=0, tiled=True)
+    full_far = jnp.concatenate(
+        lax.all_to_all(jnp.stack([far_share] * lax.axis_size("row")), "row", 0, 0), axis=0
+    )
     pp = jnp.where(column_alive, pp_occupation[0], 0)
     ph = jnp.zeros((state_count,), jnp.int32).at[ph_order[0]].set(ph_occupation[0])
     ph = jnp.where(column_alive, ph, 0)

time: 353 us -> 470 us (1.33)
  waiting for transfers between devices: 167 us -> 260 us
  matrix products: 36 us -> 45.1 us
  starting transfers between devices: 13.6 us -> 22 us
    all_gather x1, waiting for transfers between devices: 46.6 us -> 176 us  [on_device(): full_own = lax.all_gather(own_share, 'row', axis=0, tiled=True)]
    all_gather x1 -> x0, waiting for transfers between devices: 86.2 us -> none  [on_device(): full_far = lax.all_gather(far_share, 'row', axis=0, tiled=True)]
    all_to_all x0 -> x1, waiting for transfers between devices: none -> 51.8 us  [on_device(): lax.all_to_all(jnp.stack([far_share] * lax.axis_size('row')), 'row', 0, 0)]
    dot_general x3, matrix products: 13.3 us -> 22.8 us  [on_device(): jnp.dot(mix(wide, far_set), full_far, preferred_element_type=jnp.float32)]
    all_to_all x0 -> x1, starting transfers between devices: none -> 8.46 us  [on_device(): lax.all_to_all(jnp.stack([far_share] * lax.axis_size('row')), 'row', 0, 0)]
    another operation x0 -> x1, local copies, waits for them, and re-layouts: none -> 5.98 us  [on_device(): jnp.stack([far_share] * lax.axis_size('row'))]
  transfers between devices with their start and end apart: 7 -> 7, of which waited for: 5 -> 4; matrix products, arithmetic and copies ran while one was open for 8% -> 7% of each run, Pallas kernels for 0% -> 0%
where the time goes in v1:
time: 470 us; the launch traced here: 469 us
  waiting for transfers between devices  260 us (55%)
  blocking collectives  55.1 us (12%)
  local copies, waits for them, and re-layouts  48.2 us (10%)
  matrix products  45.1 us (10%)
  between operations  24.3 us (5%)
  starting transfers between devices  22 us (5%)
  other arithmetic  14 us (3%)
    all_gather x1, waiting for transfers between devices, on_device(): full_own = lax.all_gather(own_share, 'row', axis=0, tiled=True)  176 us
    all_to_all x2, blocking collectives, on_device(): lax.all_to_all(sent, ('row', 'hi'), split_axis=0, concat_axis=0, tiled=True)  55.1 us
    all_to_all x1, waiting for transfers between devices, on_device(): lax.all_to_all(jnp.stack([far_share] * lax.axis_size('row')), 'row', 0, 0)  51.8 us
    dot_general x3, matrix products, on_device(): jnp.dot(mix(wide, far_set), full_far, preferred_element_type=jnp.float32)  22.8 us
    dot_general x3, matrix products, on_device(): jnp.dot(mix(wide, own_set), full_own, preferred_element_type=jnp.float32)  22.3 us
    ppermute x4, waiting for transfers between devices, swapped(): return lax.ppermute(value, 'hi', [(0, 1), (1, 0)])  18.5 us
    all_to_all x1, waiting for transfers between devices, on_device(): lax.all_to_all(blocks, ('hi', 'row'), split_axis=0, concat_axis=0, tiled=...  13.7 us
    convert_element_type x4, local copies, waits for them, and re-layouts, on_device(): flipped.astype(jnp.float32)  12.8 us
  transfers between devices with their start and end apart: 7, of which 4 were waited for; matrix products, arithmetic and copies ran while one was open for 7% of the time, Pallas kernels for 0%

profile of v1, /device:TPU:0, one launch (start us, length us, event | category | flops | bytes accessed | tf_op | source)
XLA Modules:
  0.0 469.0 jit_solution(8768343203140598625)
XLA Ops:
  7.2 2.8 and_select_fusion.1
  10.0 3.2 collective-permute-start.2
  13.2 18.5 %collective-permute-done.2 = bf16[160,2560]{1,0:T(8,128)(2,1)S(1)} collective-permute-done((bf16[160,2560]{1,0:T(8,128)(2,1)}, bf16[160,2560]{1,0:T(8,128)(2,1)S(1)}, u32[]{:S(2)}, u32[]{:S(2)}) %collective-permute-start.2) | collective-permute-done | bytes 819232 | tf_op jit(solution)/shard_map/ppermute | solution.py:10
  31.7 6.0 %stack.14 = bf16[16,160,2560]{2,1,0:T(8,128)(2,1)} broadcast(bf16[160,2560]{1,0:T(8,128)(2,1)S(1)} %collective-permute-done.2), dimensions={1,2} | broadcast | bytes 13926400 | tf_op jit(solution)/shard_map/stack | solution.py:35
  37.7 8.5 %all-to-all-start = ((bf16[16,160,2560]{2,1,0:T(8,128)(2,1)}), bf16[16,160,2560]{2,1,0:T(8,128)(2,1)}, u32[]{:S(2)}, u32[]{:S(2)}) async-start(bf16[16,160,2560]{2,1,0:T(8,128)(2,1)} %stack.14), calls=%async_computation | async-start | bytes 26214400 | tf_op jit(solution)/shard_map/all_to_all | solution.py:35
  46.2 9.9 %scatter_custom_fusion = s32[2560]{0:T(1024)S(1)} fusion(s32[2560]{0:T(1024)S(1)} %fusion.31, s32[2560]{0:T(1024)S(1)} %reduce.1, s32[]{:T(128)} %constant.13.clone.1), kind=kCustom, calls=%fused_computation.88 | custom fusion | bytes 10244 | tf_op jit(solution)/shard_map/scatter | solution.py:38
  56.3 3.1 collective-permute-start.1
  71.7 176.4 %all-gather.2.cloned.1.call-done = bf16[2560,2560]{1,0:T(8,128)(2,1)} async-done(((bf16[160,2560]{1,0:T(8,128)(2,1)}), bf16[2560,2560]{1,0:T(8,128)(2,1)}) %all-gather.2.cloned.1.call-update) | async-done | bytes 13107216 | tf_op jit(solution)/shard_map/all_gather | solution.py:33
  248.1 8.2 %fusion.10 = f32[160,2560]{1,0:T(8,128)} fusion(bf16[2560,2560]{1,0:T(8,128)(2,1)} %all-gather.2.cloned.1.call-done, bf16[80,2560]{1,0:T(8,128)(2,1)S(1)} %get-tuple-element.26, bf16[80,2560]{1,0:T(8,128)(2,1)S(1)} %get-tuple-element.25), kind=kOutput, calls=%fused_computation.26 | convolution fusion | flops 2098790400 | bytes 15564800 | tf_op jit(solution)/shard_map/dot_general | solution.py:67
  256.3 51.8 %all-to-all-done = bf16[16,160,2560]{2,1,0:T(8,128)(2,1)} async-done(((bf16[16,160,2560]{2,1,0:T(8,128)(2,1)}), bf16[16,160,2560]{2,1,0:T(8,128)(2,1)}, u32[]{:S(2)}, u32[]{:S(2)}) %all-to-all-start) | async-done | bytes 13107232 | tf_op jit(solution)/shard_map/all_to_all | solution.py:35
  308.1 7.4 %fusion = bf16[160,2560]{1,0:T(8,128)(2,1)S(1)} fusion(f32[160,2560]{1,0:T(8,128)} %fusion.10, bf16[2560,2560]{1,0:T(8,128)(2,1)} %bitcast.8, bf16[80,2560]{1,0:T(8,128)(2,1)S(1)} %get-tuple-element.24, bf16[80,2560]{1,0:T(8,128)(2,1)S(1)} %get-tuple-element.23), kind=kOutput, calls=%fused_computation.4 | convolution fusion | flops 2099609600 | bytes 16384000 | tf_op jit(solution)/shard_map/dot_general | solution.py:69
  317.7 31.8 %all_to_all.32 = bf16[32,80,160]{1,2,0:T(8,128)(2,1)S(1)} all-to-all(bf16[32,80,160]{1,2,0:T(8,128)(2,1)S(1)} %copy.14), channel_id=1, replica_groups=mesh['hi'=2,'lo'=4,'row'=16] {'row','hi'}, dimensions={0} | all-to-all | bytes 1638400 | tf_op jit(solution)/shard_map/all_to_all | solution.py:73
  349.5 2.7 copy.15
  352.2 2.9 reshape.149
  355.7 7.0 %fusion.17 = f32[160,2560]{1,0:T(8,128)S(1)} fusion(bf16[2560,2560]{1,0:T(8,128)(2,1)} %all-gather.2.cloned.1.call-done, bf16[80,2560]{1,0:T(8,128)(2,1)S(1)} %get-tuple-element.22, bf16[80,2560]{1,0:T(8,128)(2,1)S(1)} %get-tuple-element.21), kind=kOutput, calls=%fused_computation.33 | convolution fusion | flops 2098790400 | bytes 15564800 | tf_op jit(solution)/shard_map/dot_general | solution.py:67
  362.8 7.0 %fusion.1 = bf16[160,2560]{1,0:T(8,128)(2,1)S(1)} fusion(f32[160,2560]{1,0:T(8,128)S(1)} %fusion.17, bf16[2560,2560]{1,0:T(8,128)(2,1)} %bitcast.8, bf16[80,2560]{1,0:T(8,128)(2,1)S(1)} %get-tuple-element.20, bf16[80,2560]{1,0:T(8,128)(2,1)S(1)} %get-tuple-element.19), kind=kOutput, calls=%fused_computation.5 | convolution fusion | flops 2099609600 | bytes 16384000 | tf_op jit(solution)/shard_map/dot_general | solution.py:69
  369.8 2.4 all_to_all.24
  372.2 1.8 copy.16
  374.1 23.2 %all_to_all.33 = bf16[32,80,160]{1,2,0:T(8,128)(2,1)S(1)} all-to-all(bf16[32,80,160]{1,2,0:T(8,128)(2,1)S(1)} %copy.16), channel_id=1, replica_groups=mesh['hi'=2,'lo'=4,'row'=16] {'row','hi'}, dimensions={0} | all-to-all | bytes 1638400 | tf_op jit(solution)/shard_map/all_to_all | solution.py:73
  397.3 1.8 convert_bitcast_fusion
  399.1 4.3 copy.17
  403.4 2.9 reshape.150
  408.1 7.1 %fusion.24 = f32[160,2560]{1,0:T(8,128)S(1)} fusion(bf16[2560,2560]{1,0:T(8,128)(2,1)} %all-gather.2.cloned.1.call-done, bf16[80,2560]{1,0:T(8,128)(2,1)S(1)} %get-tuple-element.18, bf16[80,2560]{1,0:T(8,128)(2,1)S(1)} %get-tuple-element.17), kind=kOutput, calls=%fused_computation.40 | convolution fusion | flops 2098790400 | bytes 15564800 | tf_op jit(solution)/shard_map/dot_general | solution.py:67
  415.3 8.3 %multiply_subtract_fusion = (f32[160,2560]{1,0:T(8,128)S(1)}, bf16[160,2560]{1,0:T(8,128)(2,1)}) fusion(f32[160,2560]{1,0:T(8,128)S(1)} %reshape.149, bf16[160,2560]{1,0:T(8,128)(2,1)S(1)} %copy-done.1, f32[160,2560]{1,0:T(8,128)S(1)} %reshape.150, bf16[160,2560]{1,0:T(8,128)(2,1)S(1)} %copy-done.3, f32[160,2560]{1,0:T(8,128)S(1)} %fusion.24, ...), kind=kOutput, calls=%fused_computation.13 | convolution fusion | flops 2104115200 | bytes 22937600 | tf_op jit(solution)/shard_map/dot_general | solution.py:69
  424.8 2.6 reshape.148
  427.4 2.3 copy.18
  429.6 6.0 %all-to-all-start.3 = ((bf16[32,160,80]{2,1,0:T(8,128)(2,1)}), bf16[32,160,80]{2,1,0:T(8,128)(2,1)S(1)}, u32[]{:S(2)}, u32[]{:S(2)}) async-start(bf16[32,160,80]{2,1,0:T(8,128)(2,1)} %bitcast.18), calls=%async_computation.3 | async-start | bytes 2621440 | tf_op jit(solution)/shard_map/all_to_all | solution.py:85
  435.6 2.4 fusion.7
  438.0 13.7 %all-to-all-done.3 = bf16[32,160,80]{2,1,0:T(8,128)(2,1)S(1)} async-done(((bf16[32,160,80]{2,1,0:T(8,128)(2,1)}), bf16[32,160,80]{2,1,0:T(8,128)(2,1)S(1)}, u32[]{:S(2)}, u32[]{:S(2)}) %all-to-all-start.3) | async-done | bytes 819232 | tf_op jit(solution)/shard_map/all_to_all | solution.py:85
  452.0 2.0 copy.19
  454.0 4.7 %div.26 = f32[1,160,2560]{2,1,0:T(8,128)} reshape(f32[160,16,2,80]{3,2,1,0:T(2,128)S(1)} %copy.19) | data formatting | bytes 3276800 | tf_op jit(solution)/shard_map/div | solution.py:89
  458.7 3.5 fusion.3
  (56 shorter events, 8.5 us)
Async XLA Ops:
  6.5 241.6 %all-gather.2.cloned.1.call-start = ((), (), s32[]{:S(2)}) async-start(), calls=%async_computation.4 | async-start | bytes 13926400 | tf_op jit(solution)/shard_map/all_gather | solution.py:33
  10.0 21.7 %collective-permute-start.2 = (bf16[160,2560]{1,0:T(8,128)(2,1)}, bf16[160,2560]{1,0:T(8,128)(2,1)S(1)}, u32[]{:S(2)}, u32[]{:S(2)}) collective-permute-start(bf16[160,2560]{1,0:T(8,128)(2,1)} %get-tuple-element.38), channel_id=1, source_target_pairs={{0,64},{64,0},{1,65},{65,1},{2,66},{66,2},{3,67},{67,3},{4,68},{68... | collective-permute-start | bytes 2457608 | tf_op jit(solution)/shard_map/ppermute | solution.py:10
  37.7 8.5 %copy-start.7 = (s32[1,2560]{1,0:T(1,128)S(1)}, s32[1,2560]{1,0:T(1,128)}, u32[]{:S(2)}) copy-start(s32[1,2560]{1,0:T(1,128)} %param.11) | copy-start | bytes 30724
  37.7 8.5 %copy-start.8 = (s32[1,2560]{1,0:T(1,128)S(1)}, s32[1,2560]{1,0:T(1,128)}, u32[]{:S(2)}) copy-start(s32[1,2560]{1,0:T(1,128)} %param.12) | copy-start | bytes 30724
  37.7 18.5 %copy-start.9 = (s32[1,2560]{1,0:T(1,128)S(1)}, s32[1,2560]{1,0:T(1,128)}, u32[]{:S(2)}) copy-start(s32[1,2560]{1,0:T(1,128)} %param.10) | copy-start | bytes 30724
  37.7 22.3 %copy-start.10 = (f32[8,2]{0,1:T(2,128)S(1)}, f32[8,2]{0,1:T(2,128)}, u32[]{:S(2)}) copy-start(f32[8,2]{0,1:T(2,128)} %param.13) | copy-start | bytes 196
  37.7 270.4 %all-to-all-start = ((bf16[16,160,2560]{2,1,0:T(8,128)(2,1)}), bf16[16,160,2560]{2,1,0:T(8,128)(2,1)}, u32[]{:S(2)}, u32[]{:S(2)}) async-start(bf16[16,160,2560]{2,1,0:T(8,128)(2,1)} %stack.14), calls=%async_computation | async-start | bytes 26214400 | tf_op jit(solution)/shard_map/all_to_all | solution.py:35
  56.3 14.3 %collective-permute-start.1 = (f32[2,2560]{1,0:T(2,128)S(1)}, f32[2,2560]{1,0:T(2,128)S(1)}, u32[]{:S(2)}, u32[]{:S(2)}) collective-permute-start(f32[2,2560]{1,0:T(2,128)S(1)} %add_convert_fusion.12), channel_id=1, source_target_pairs={{0,64},{64,0},{1,65},{65,1},{2,66},{66,2},{3,67},{67,3},{4,68},{68... | collective-permute-start | bytes 61448 | tf_op jit(solution)/shard_map/ppermute | solution.py:10
  59.4 11.6 %collective-permute-start = (bf16[80,2560]{1,0:T(8,128)(2,1)S(1)}, bf16[80,2560]{1,0:T(8,128)(2,1)S(1)}, u32[]{:S(2)}, u32[]{:S(2)}) collective-permute-start(bf16[80,2560]{1,0:T(8,128)(2,1)S(1)} %constant_dynamic-slice_fusion.2), channel_id=1, source_target_pairs={{0,64},{64,0},{1,65},{65,1},{2,66},{66,2},{3,67},{67,3},{4,68},{68... | collective-permute-start | bytes 1228808 | tf_op jit(solution)/shard_map/ppermute | solution.py:10
  315.5 39.6 %copy-start = (bf16[160,2560]{1,0:T(8,128)(2,1)}, bf16[160,2560]{1,0:T(8,128)(2,1)S(1)}, u32[]{:S(2)}) copy-start(bf16[160,2560]{1,0:T(8,128)(2,1)S(1)} %fusion) | copy-start | bytes 2457604
  369.8 4.3 copy-start.2
  408.1 7.2 %copy-start.1 = (bf16[160,2560]{1,0:T(8,128)(2,1)S(1)}, bf16[160,2560]{1,0:T(8,128)(2,1)}, u32[]{:S(2)}) copy-start(bf16[160,2560]{1,0:T(8,128)(2,1)} %copy-done) | copy-start | bytes 2457604
  408.1 7.2 %copy-start.3 = (bf16[160,2560]{1,0:T(8,128)(2,1)S(1)}, bf16[160,2560]{1,0:T(8,128)(2,1)}, u32[]{:S(2)}) copy-start(bf16[160,2560]{1,0:T(8,128)(2,1)} %copy-done.2) | copy-start | bytes 2457604
  423.6 1.2 copy-start.4
  423.6 12.0 %collective-permute-start.3 = (bf16[80,2560]{1,0:T(8,128)(2,1)S(1)}, bf16[80,2560]{1,0:T(8,128)(2,1)}, u32[]{:S(2)}, u32[]{:S(2)}) collective-permute-start(bf16[80,2560]{1,0:T(8,128)(2,1)S(1)} %dynamic-slice_convert_fusion), channel_id=1, source_target_pairs={{0,64},{64,0},{1,65},{65,1},{2,66},{66,2},{3,67},{67,3},{4,68},{68... | collective-permute-start | bytes 1228808 | tf_op jit(solution)/shard_map/ppermute | solution.py:10
  429.6 6.0 %copy-start.5 = (f32[160,2560]{1,0:T(8,128)S(1)}, f32[160,2560]{1,0:T(8,128)}, u32[]{:S(2)}) copy-start(f32[160,2560]{1,0:T(8,128)} %copy-done.4) | copy-start | bytes 4915204
  429.6 22.0 %all-to-all-start.3 = ((bf16[32,160,80]{2,1,0:T(8,128)(2,1)}), bf16[32,160,80]{2,1,0:T(8,128)(2,1)S(1)}, u32[]{:S(2)}, u32[]{:S(2)}) async-start(bf16[32,160,80]{2,1,0:T(8,128)(2,1)} %bitcast.18), calls=%async_computation.3 | async-start | bytes 2621440 | tf_op jit(solution)/shard_map/all_to_all | solution.py:85
  454.0 4.7 %copy-start.6 = (bf16[1,160,2560]{2,1,0:T(8,128)(2,1)S(1)}, bf16[1,160,2560]{2,1,0:T(8,128)(2,1)}, u32[]{:S(2)}) copy-start(bf16[1,160,2560]{2,1,0:T(8,128)(2,1)} %param.8) | copy-start | bytes 2457604
Sparse Core Ops, SparseCore 0:
  10.1 237.9 all-gather.1
